TPU v7x, 128 devices: a whole 4x4x4 slice. The times are simulated.
128 devices in a mesh: replica: 4 (over z), shard: 16 (over y, x_lo, core), tensor: 2 (over x_hi).
Axes of the slice: x: 4 (x_hi: 2, x_lo: 2; x = x_hi * 2 + x_lo), y: 4, z: 4, core: 2. Of those that a mesh axis runs over, the one named last changes fastest.
Arguments:
- trained_up: bfloat16 [4, 1024, 4096], P('replica', None, 'tensor'), may hold values from -6 to 6
- trained_down: bfloat16 [4, 4096, 1024], P('replica', 'tensor'), may hold values from -6 to 6
- trained_embed: bfloat16 [4, 32768, 1024], P('replica', ('shard', 'tensor')), may hold values from -6 to 6
- trained_norm: bfloat16 [4, 2, 1024], P('replica'), may hold values from 0.099609375 to 1.8984375
- master_up: float32 [1024, 4096], P(('replica', 'shard', 'tensor')), may hold values from -6 to 6
- moment_up: float32 [1024, 4096], P(('replica', 'shard', 'tensor')), may hold values from -4 to 4
- master_down: float32 [2, 2048, 1024], P('tensor', ('replica', 'shard')), may hold values from -6 to 6
- moment_down: float32 [2, 2048, 1024], P('tensor', ('replica', 'shard')), may hold values from -4 to 4
- master_embed: float32 [32, 1024, 1024], P(('shard', 'tensor'), 'replica'), may hold values from -6 to 6
- moment_embed: float32 [32, 1024, 64], P(('shard', 'tensor'), 'replica'), may hold values from -4 to 4
- master_norm: float32 [2, 1024], replicated, may hold values from 0.1 to 1.9
- moment_norm: float32 [2, 1024], replicated, may hold values from -2 to 2
- embed_basis: float32 [1024, 64], replicated, may hold values from -0.1875 to 0.1875
Outputs:
- recast_up: bfloat16 [1024, 4096], P(None, 'tensor')
- recast_down: bfloat16 [4096, 1024], P('tensor')
- recast_embed: bfloat16 [32768, 1024], P(('shard', 'tensor'))
- recast_norm: bfloat16 [2, 1024], replicated
- stored_up: float32 [1024, 4096], P(('replica', 'shard', 'tensor'))
- velocity_up: float32 [1024, 4096], P(('replica', 'shard', 'tensor'))
- stored_down: float32 [2, 2048, 1024], P('tensor', ('replica', 'shard'))
- velocity_down: float32 [2, 2048, 1024], P('tensor', ('replica', 'shard'))
- stored_embed: float32 [32, 1024, 1024], P(('shard', 'tensor'), 'replica')
- velocity_embed: float32 [32, 1024, 64], P(('shard', 'tensor'), 'replica')
- stored_norm: float32 [2, 1024], replicated
- velocity_norm: float32 [2, 1024], replicated
All inputs are finite; a program needn't handle non-finite values.
Results may differ from a plain program's by a relative error of at most 0.012.
Values may be sent and summed in bfloat16 or wider, within the bound.
A program may use at most 128 MiB of HBM per device.

v0:
```python
import jax
import jax.numpy as jnp
from jax import lax
from jax.sharding import PartitionSpec as P


def outer_step(master, moment, summed, groups):
    difference = master - summed / groups
    velocity = 0.5 * moment + difference
    return (master - 0.7 * (difference + 0.5 * velocity), velocity)


def body(
    trained_up,
    trained_down,
    trained_embed,
    trained_norm,
    master_up,
    moment_up,
    master_down,
    moment_down,
    master_embed,
    moment_embed,
    master_norm,
    moment_norm,
    embed_basis,
):
    replicas = lax.axis_size("replica")
    shards = lax.axis_size("shard")
    tensors = lax.axis_size("tensor")
    shard_pos = lax.axis_index("shard")
    width = embed_basis.shape[0]
    rows_up = master_up.shape[0]
    half_cols = trained_up.shape[2]
    rows_down = master_down.shape[1]
    up_blocks = trained_up[0].reshape(replicas, shards, tensors, rows_up, half_cols)
    up_own = lax.dynamic_index_in_dim(up_blocks, shard_pos, 1, keepdims=False)
    down_blocks = trained_down[0].reshape(replicas, shards, rows_down, width)
    down_own = lax.dynamic_index_in_dim(down_blocks, shard_pos, 1, keepdims=False)
    up_summed, down_summed = (
        lax.psum_scatter(
            up_own.astype(jnp.float32).astype(jnp.bfloat16),
            "replica",
            scatter_dimension=0,
            tiled=True,
        ).astype(jnp.float32),
        lax.psum_scatter(
            down_own.astype(jnp.float32).astype(jnp.bfloat16),
            "replica",
            scatter_dimension=0,
            tiled=True,
        ).astype(jnp.float32),
    )
    up_summed = lax.all_to_all(up_summed, "tensor", split_axis=1, concat_axis=3, tiled=True)
    stored_up, velocity_up = outer_step(
        master_up, moment_up, up_summed.reshape(rows_up, half_cols * tensors), replicas
    )
    stored_down, velocity_down = outer_step(master_down, moment_down, down_summed, replicas)
    norm_summed = lax.psum(trained_norm[0].astype(jnp.float32), "replica")
    stored_norm, velocity_norm = outer_step(master_norm, moment_norm, norm_summed, replicas)
    embed_own = master_embed[0]
    rows_embed = embed_own.shape[0]
    embed_terms = trained_embed[0].reshape(replicas, rows_embed, width).astype(jnp.float32)
    embed_summed = lax.psum_scatter(
        embed_terms.astype(jnp.bfloat16), "replica", scatter_dimension=0, tiled=True
    ).astype(jnp.float32)[0]
    coefficient = jnp.dot(
        embed_own - embed_summed / replicas, embed_basis, precision=lax.Precision.HIGHEST
    )
    velocity_rows = 0.5 * moment_embed[0] + coefficient
    stored_rows = embed_own - 0.7 * jnp.dot(
        coefficient + 0.5 * velocity_rows, embed_basis.T, precision=lax.Precision.HIGHEST
    )
    up_piece = lax.all_to_all(
        stored_up.astype(jnp.bfloat16), "tensor", split_axis=1, concat_axis=0, tiled=True
    )
    down_piece = stored_down[0].astype(jnp.bfloat16)
    recast_up, recast_down = (
        lax.all_gather(up_piece, ("replica", "shard"), axis=0, tiled=True),
        lax.all_gather(down_piece, ("replica", "shard"), axis=0, tiled=True),
    )
    recast_embed = lax.all_gather(stored_rows.astype(jnp.bfloat16), "replica", axis=0, tiled=True)
    return (
        recast_up,
        recast_down,
        recast_embed,
        stored_norm.astype(jnp.bfloat16),
        stored_up,
        velocity_up,
        stored_down,
        velocity_down,
        stored_rows[None],
        velocity_rows[None],
        stored_norm,
        velocity_norm,
    )


def solution(mesh):
    in_specs = (
        P("replica", None, "tensor"),
        P("replica", "tensor", None),
        P("replica", ("shard", "tensor"), None),
        P("replica", None, None),
        P(("replica", "shard", "tensor"), None),
        P(("replica", "shard", "tensor"), None),
        P("tensor", ("replica", "shard"), None),
        P("tensor", ("replica", "shard"), None),
        P(("shard", "tensor"), "replica", None),
        P(("shard", "tensor"), "replica", None),
        P(),
        P(),
        P(),
    )
    out_specs = (
        P(None, "tensor"),
        P("tensor", None),
        P(("shard", "tensor"), None),
        P(),
        P(("replica", "shard", "tensor"), None),
        P(("replica", "shard", "tensor"), None),
        P("tensor", ("replica", "shard"), None),
        P("tensor", ("replica", "shard"), None),
        P(("shard", "tensor"), "replica", None),
        P(("shard", "tensor"), "replica", None),
        P(),
        P(),
    )
    return jax.shard_map(body, mesh=mesh, in_specs=in_specs, out_specs=out_specs, check_vma=False)
```

profile of v0, /device:TPU:1, one launch (start us, length us, event | category | flops | bytes accessed | tf_op | source)
XLA Modules:
  0.0 376.6 jit_solution(8853071086595991756)
XLA Ops:
  7.2 0.0 copy-start
  7.2 0.0 copy-start.1
  7.2 0.0 copy-start.4
  7.2 0.0 reduce-scatter.6.cloned.1.call-start
  7.3 0.0 copy-start.12
  7.3 0.7 reduce-scatter.6.cloned.1.call-update
  7.9 0.0 copy-start.7
  8.0 0.0 copy-start.8
  8.0 0.0 all-reduce.3.cloned.1.call-start
  8.0 1.7 copy_bitcast_fusion
  9.7 0.0 all-reduce.3.cloned.1.call-update
  9.7 0.0 reduce-scatter.4.cloned.1.call-start
  9.8 0.0 copy-start.11
  9.8 1.7 dynamic-slice_bitcast_fusion
  11.5 0.0 reduce-scatter.4.cloned.1.call-update
  11.5 0.0 all-gather.7.cloned.1.call-start
  11.6 32.1 %reduce-scatter.6.cloned.1.call-done = bf16[1,256,1024]{2,1,0:T(8,128)(2,1)} async-done(((bf16[4,256,1024]{2,1,0:T(8,128)(2,1)}), bf16[1,256,1024]{2,1,0:T(8,128)(2,1)}) %reduce-scatter.6.cloned.1.call-update) | async-done | bytes 524304 | tf_op jit(solution)/shard_map/reduce_scatter | solution.py:64
  43.6 0.0 copy-done
  43.6 0.0 copy-done.1
  43.6 2.2 fusion.1
  45.8 0.0 copy-done.4
  45.8 2.2 fusion.16
  48.0 0.0 all-gather.7.cloned.1.call-update
  48.1 0.0 all-gather.5.cloned.1.call-start
  48.1 0.0 copy-done.12
  48.1 0.6 dynamic-slice
  48.7 37.3 %all-reduce.3.cloned.1.call-done = bf16[4,2,8,2048]{3,2,0,1:T(8,128)(2,1)} async-done(((bf16[4,2,8,2048]{3,2,0,1:T(8,128)(2,1)}), bf16[4,2,8,2048]{3,2,0,1:T(8,128)(2,1)}) %all-reduce.3.cloned.1.call-update) | async-done | bytes 262160
  86.0 1.5 dynamic-slice_convert_fusion
  87.5 8.6 %all_to_all.28 = f32[1,2,8,2048]{3,2,0,1:T(8,128)S(1)} all-to-all(f32[1,2,8,2048]{3,2,0,1:T(8,128)S(1)} %dynamic-slice_convert_fusion), channel_id=1, replica_groups=mesh['replica'=4,'shard'=16,'tensor'=2] {'tensor'}, dimensions={1} | all-to-all | bytes 262144 | tf_op jit(solution)/shard_map/all_to_all | solution.py:54
  96.1 0.7 fusion.15
  96.9 7.5 %all_to_all.29 = bf16[8,2,2048]{2,0,1:T(8,128)(2,1)} all-to-all(bf16[8,2,2048]{2,0,1:T(8,128)(2,1)S(1)} %bitcast.53), channel_id=1, replica_groups=mesh['replica'=4,'shard'=16,'tensor'=2] {'tensor'}, dimensions={1} | all-to-all | bytes 131072 | tf_op jit(solution)/shard_map/all_to_all | solution.py:74
  104.4 0.0 all-gather.5.cloned.1.call-update
  104.4 0.0 all-gather.9.cloned.1.call-start
  104.4 5.8 %reduce-scatter.4.cloned.1.call-done = bf16[1,32,1024]{2,1,0:T(8,128)(2,1)} async-done(((bf16[4,32,1024]{2,1,0:T(8,128)(2,1)}), bf16[1,32,1024]{2,1,0:T(8,128)(2,1)}) %reduce-scatter.4.cloned.1.call-update) | async-done | bytes 65552 | tf_op jit(solution)/shard_map/reduce_scatter | solution.py:47
  110.3 0.0 copy-done.6
  110.3 1.6 fusion.14
  111.9 0.0 all-gather.9.cloned.1.call-update
  111.9 6.9 %psum.7 = f32[2,1024]{1,0:T(2,128)S(1)} all-reduce(f32[2,1024]{1,0:T(2,128)S(1)} %bitcast_convert_fusion), channel_id=1, replica_groups=mesh['replica'=4,'shard'=16,'tensor'=2] {'replica'}, use_global_device_ids=true, to_apply=%region_3.4 | all-reduce | flops 2048 | bytes 16384 | tf_op jit(solution)/shard_map/psum | solution.py:59
  118.9 0.6 fusion.13
  119.5 0.6 fusion.8
  120.2 25.0 %all-gather.7.cloned.1.call-done = bf16[1024,1024]{1,0:T(8,128)(2,1)} async-done(((bf16[256,1024]{1,0:T(8,128)(2,1)}), bf16[1024,1024]{1,0:T(8,128)(2,1)}) %all-gather.7.cloned.1.call-update) | async-done | bytes 2097168 | tf_op jit(solution)/shard_map/all_gather | solution.py:82
  145.2 108.0 %all-gather.5.cloned.1.call-done = bf16[1024,2048]{1,0:T(8,128)(2,1)} async-done(((bf16[16,2048]{1,0:T(8,128)(2,1)}), bf16[1024,2048]{1,0:T(8,128)(2,1)}) %all-gather.5.cloned.1.call-update) | async-done | bytes 4194320 | tf_op jit(solution)/shard_map/all_gather | solution.py:79
  253.2 107.3 %all-gather.9.cloned.1.call-done = bf16[1,2048,1024]{2,1,0:T(8,128)(2,1)} async-done(((bf16[1,32,1024]{2,1,0:T(8,128)(2,1)}), bf16[1,2048,1024]{2,1,0:T(8,128)(2,1)}) %all-gather.9.cloned.1.call-update) | async-done | bytes 4194320 | tf_op jit(solution)/shard_map/all_gather | solution.py:80
  360.4 4.9 %copy.39 = bf16[1024,2048]{1,0:T(8,128)(2,1)} copy(bf16[1024,2048]{1,0:T(8,128)(2,1)} %all-gather.5.cloned.1.call-done) | data formatting | bytes 8388608
  365.4 0.0 copy-done.2
  365.4 2.1 copy.40
  367.5 1.0 copy-done.3
  368.5 1.3 copy.41
  (14 shorter events, 0.0 us)
Async XLA Ops:
  7.2 36.5 %copy-start = (f32[1024,64]{0,1:T(8,128)S(1)}, f32[1024,64]{0,1:T(8,128)}, u32[]{:S(2)}) copy-start(f32[1024,64]{0,1:T(8,128)} %param.25) | copy-start | bytes 786436
  7.2 36.5 %copy-start.1 = (f32[1,256,1024]{2,1,0:T(8,128)S(1)}, f32[1,256,1024]{2,1,0:T(8,128)}, u32[]{:S(2)}) copy-start(f32[1,256,1024]{2,1,0:T(8,128)} %param.21) | copy-start | bytes 3145732
  7.2 38.6 %copy-start.4 = (f32[1,256,64]{1,2,0:T(8,128)S(1)}, f32[1,256,64]{1,2,0:T(8,128)}, u32[]{:S(2)}) copy-start(f32[1,256,64]{1,2,0:T(8,128)} %param.22) | copy-start | bytes 196612
  7.2 36.4 %reduce-scatter.6.cloned.1.call-start = ((), (), s32[]{:S(2)}) async-start(), calls=%async_computation.6 | async-start | bytes 2621440 | tf_op jit(solution)/shard_map/reduce_scatter | solution.py:64
  7.3 40.9 %copy-start.12 = (u32[128]{0:T(128)S(1)}, u32[128]{0:T(128)}, u32[]{:S(2)}) copy-start(u32[128]{0:T(128)} %constant.47) | copy-start | bytes 1540
  7.9 88.2 %copy-start.7 = (f32[8,4096]{1,0:T(8,128)S(1)}, f32[8,4096]{1,0:T(8,128)}, u32[]{:S(2)}) copy-start(f32[8,4096]{1,0:T(8,128)} %param.17) | copy-start | bytes 393220
  8.0 88.2 %copy-start.8 = (f32[8,4096]{1,0:T(8,128)S(1)}, f32[8,4096]{1,0:T(8,128)}, u32[]{:S(2)}) copy-start(f32[8,4096]{1,0:T(8,128)} %param.18) | copy-start | bytes 393220
  8.0 78.0 %all-reduce.3.cloned.1.call-start = ((), (), s32[]{:S(2)}) async-start(), calls=%async_computation.9 | async-start | bytes 524288
  9.7 100.6 %copy-start.5 = (f32[1,32,1024]{2,1,0:T(8,128)S(1)}, f32[1,32,1024]{2,1,0:T(8,128)}, u32[]{:S(2)}) copy-start(f32[1,32,1024]{2,1,0:T(8,128)} %param.19) | copy-start | bytes 393220
  9.7 100.6 %copy-start.6 = (f32[1,32,1024]{2,1,0:T(8,128)S(1)}, f32[1,32,1024]{2,1,0:T(8,128)}, u32[]{:S(2)}) copy-start(f32[1,32,1024]{2,1,0:T(8,128)} %param.20) | copy-start | bytes 393220
  9.7 100.6 %reduce-scatter.4.cloned.1.call-start = ((), (), s32[]{:S(2)}) async-start(), calls=%async_computation.5 | async-start | bytes 327680 | tf_op jit(solution)/shard_map/reduce_scatter | solution.py:47
  9.8 102.1 %copy-start.11 = (bf16[1,2,1024]{2,1,0:T(2,128)(2,1)S(1)}, bf16[1,2,1024]{2,1,0:T(2,128)(2,1)}, u32[]{:S(2)}) copy-start(bf16[1,2,1024]{2,1,0:T(2,128)(2,1)} %param.16) | copy-start | bytes 12292
  11.5 107.4 %copy-start.9 = (f32[2,1024]{1,0:T(2,128)S(1)}, f32[2,1024]{1,0:T(2,128)}, u32[]{:S(2)}) copy-start(f32[2,1024]{1,0:T(2,128)} %param.23) | copy-start | bytes 24580
  11.5 107.4 %copy-start.10 = (f32[2,1024]{1,0:T(2,128)S(1)}, f32[2,1024]{1,0:T(2,128)}, u32[]{:S(2)}) copy-start(f32[2,1024]{1,0:T(2,128)} %param.24) | copy-start | bytes 24580
  11.5 133.6 %all-gather.7.cloned.1.call-start = ((), (), s32[]{:S(2)}) async-start(), calls=%async_computation.7 | async-start | bytes 2621440 | tf_op jit(solution)/shard_map/all_gather | solution.py:82
  48.1 205.1 %all-gather.5.cloned.1.call-start = ((), (), s32[]{:S(2)}) async-start(), calls=%async_computation.4 | async-start | bytes 4259840 | tf_op jit(solution)/shard_map/all_gather | solution.py:79
  104.4 256.0 %all-gather.9.cloned.1.call-start = ((), (), s32[]{:S(2)}) async-start(), calls=%async_computation.8 | async-start | bytes 4259840 | tf_op jit(solution)/shard_map/all_gather | solution.py:80
  360.4 4.9 %copy-start.2 = (bf16[1,2048,1024]{2,1,0:T(8,128)(2,1)S(1)}, bf16[1,2048,1024]{2,1,0:T(8,128)(2,1)}, u32[]{:S(2)}) copy-start(bf16[1,2048,1024]{2,1,0:T(8,128)(2,1)} %all-gather.9.cloned.1.call-done) | copy-start | bytes 12582916
  365.4 3.1 copy-start.3
Sparse Core Ops, SparseCore 0:
  10.4 33.1 reduce-scatter.5
  46.7 39.3 all-reduce.2
  89.0 21.2 reduce-scatter.3
  112.5 32.6 all-gather.6
  146.9 106.2 all-gather.4
  255.4 104.9 all-gather.8
where the time goes:
time: 377 us
  waiting for transfers between devices  316 us (84%)
  blocking collectives  23 us (6%)
  between operations  14.3 us (4%)
  local copies, waits for them, and re-layouts  13.4 us (4%)
  other arithmetic  5.09 us (1%)
  matrix products  4.38 us (1%)
    all_gather x1, waiting for transfers between devices, body(): lax.all_gather(up_piece, ('replica', 'shard'), axis=0, tiled=True)  108 us
    all_gather x1, waiting for transfers between devices, body(): lax.all_gather(down_piece, ('replica', 'shard'), axis=0, tiled=True)  107 us
    unnamed x7, waiting for transfers between devices  38.1 us
    reduce_scatter x1, waiting for transfers between devices, body(): lax.psum_scatter(embed_terms.astype(jnp.bfloat16), 'replica', scatter_dim...  32.1 us
    all_gather x1, waiting for transfers between devices, body(): lax.all_gather(stored_rows.astype(jnp.bfloat16), 'replica', axis=0, tiled...  25 us
    unnamed x30, local copies, waits for them, and re-layouts  10 us
    all_to_all x1, blocking collectives, body(): lax.all_to_all(up_summed, 'tensor', split_axis=1, concat_axis=3, tiled=True)  8.59 us
  transfers between devices with their start and end apart: 6, of which 6 were waited for; matrix products, arithmetic and copies ran while one was open for 4% of the time, Pallas kernels for 0%

commit v1 on v0

v1 whole, which is shorter than its diff:
```python
import jax
import jax.numpy as jnp
from jax import lax
from jax.experimental import pallas as pl
from jax.experimental.pallas import tpu as pltpu
from jax.sharding import PartitionSpec as P

MESH = pl.DeviceIdType.MESH
F32, BF16 = jnp.float32, jnp.bfloat16

ORDER = [
    "D030", "D010", "D001", "D300", "D100", "U001", "U030", "U010", "U300", "U100",
    "m1", "pw",
    "D020", "D031", "D310", "D011", "D330", "D110", "D200", "D301", "D130", "r0",
    "U011", "D101", "U031", "U310", "U020", "D021", "U110", "U301", "U101",
    "m2", "m3", "U330", "D311", "U200", "D320", "x", "U130", "D331", "D120", "D111", "D230", "D210",
    "D201", "U331", "U021", "r1", "D131", "U131", "U201", "e0", "U320", "U230", "D321", "U120", "D121", "D220",
    "U311", "D231", "e1", "U321", "U111", "D211", "U121", "U210", "U220", "D221", "U211", "U231", "U221",
]


def routes(kind, o, p, e):
    every_y = [("y+", ""), ("y-", "")]
    if kind == "D":
        if p == 0 and e == 0:
            z_part = {0: [("z+", ""), ("z-", "")], 3: [("z+", "a")], 1: [("z-", "b")], 2: []}[o]
            return z_part + every_y + [("x", ""), ("c", "")]
        if e == 0:
            relay = [("y+", "")] if p == 3 and o % 2 == 0 else [("y-", "")] if p == 1 and o % 2 == 1 else []
            return relay + [("x", ""), ("c", "")]
        return [("c", "")]
    if p == 0:
        x_part = [("x", "")] if o == 0 and e == 0 else []
        z_part = {0: [("z+", ""), ("z-", "")], 3: [("z+", "a")], 1: [("z-", "b")], 2: []}[o]
        return x_part + z_part + every_y + [("c", "")]
    odd = (o + e) % 2
    relay = [("y+", "")] if p == 3 and not odd else [("y-", "")] if p == 1 and odd else []
    return relay + [("c", "")]


def seen_from(direction, o, p, e):
    if direction == "z+":
        return (o + 3) % 4, p, e
    if direction == "z-":
        return (o + 1) % 4, p, e
    if direction == "y+":
        return o, (p + 3) % 4, e
    if direction == "y-":
        return o, (p + 1) % 4, e
    if direction == "x":
        return o, p, 1 - e
    return o, p, e


def outer_step(master, moment, summed):
    difference = master - summed * 0.25
    velocity = 0.5 * moment + difference
    return master - 0.7 * (difference + 0.5 * velocity), velocity


def nt_dot(a, b):
    return lax.dot_general(a, b, (((1,), (1,)), ((), ())), preferred_element_type=F32)


SLOTS = {}


def slot(key):
    return SLOTS.setdefault(key, len(SLOTS))


N_RECV = 104
N_SEND = 56


def exchange(
    tu, td, te, tn, mu, vu, md, vd, me, ve, mn, vn, bt,
    RU, RD, RE, RN, SU, VU, SD, VD, SE, VE, SN, VN,
    tu_v, td_v, te_v, nb, mu_v, vu_v, md_v, vd_v, m_v, ve_v, mn_v, vn_v, bt_v,
    ru_a, ru_m, ru_p, rd_a, rd_m, rd_p, su, sd, cs, cr, xs, xr, so,
    bs, mb, pf, pp, pr, wv, ms,
    lsem, ssem, gsem, rsem, csem,
):
    SLOTS.clear()
    z, s, t = lax.axis_index("replica"), lax.axis_index("shard"), lax.axis_index("tensor")
    y, x, c = lax.div(s, 4), lax.rem(lax.div(s, 2), 2), lax.rem(s, 2)
    zo = [z] + [lax.rem(z + i, 4) for i in (1, 2, 3)]
    yo = [y] + [lax.rem(y + i, 4) for i in (1, 2, 3)]
    xo = [x, 1 - x]
    devices = {
        "z+": (zo[1], s, t),
        "z-": (zo[3], s, t),
        "z2": (zo[2], s, t),
        "y+": (z, yo[1] * 4 + x * 2 + c, t),
        "y-": (z, yo[3] * 4 + x * 2 + c, t),
        "x": (z, y * 4 + xo[1] * 2 + c, t),
        "c": (z, y * 4 + x * 2 + (1 - c), t),
        "t": (z, s, 1 - t),
    }

    def block(o, p, e, core=c):
        return zo[o] * 16 + yo[p] * 4 + xo[e] * 2 + core

    loads = {}

    def load(name, src, dst):
        loads[name] = pltpu.make_async_copy(src, dst, lsem.at[len(loads)])
        loads[name].start()

    load("tu", tu.at[:, s], tu_v)
    load("td", td.at[:, s], td_v)
    load("mu", mu, mu_v)
    load("vu", vu, vu_v)
    load("md", md, md_v)
    load("vd", vd, vd_v)
    load("tn", tn, nb.at[z])
    load("me", me, m_v)
    load("bt", bt, bt_v)
    load("te", te, te_v)
    load("ve", ve, ve_v)
    load("mn", mn, mn_v)
    load("vn", vn, vn_v)

    barrier = pltpu.get_barrier_semaphore()
    for device in devices.values():
        pl.semaphore_signal(barrier, inc=1, device_id=device, device_id_type=MESH)
    pl.semaphore_wait(barrier, len(devices))

    single = []
    grouped = {}
    group_index = {"z+": 0, "z-": 1, "y+": 2, "y-": 3, "x": 4, "c": 5}

    def push(src, dst, key, direction):
        copy = pltpu.make_async_remote_copy(
            src, dst, ssem.at[len(single)], rsem.at[slot(key)], device_id=devices[direction], device_id_type=MESH
        )
        copy.start()
        single.append(copy)

    def arrived(ref, key):
        pltpu.make_async_remote_copy(
            ref, ref, ssem.at[0], rsem.at[slot(key)], device_id=devices["c"], device_id_type=MESH
        ).wait_recv()

    gathered = {"D": RD, "U": RU}
    half_rows = {"D": 16, "U": 8}

    def half_of(kind, which, index):
        n = half_rows[kind]
        return gathered[kind].at[index, pl.ds(0 if which == "a" else n, n)]

    def forward(kind, o, p, e):
        index = block(o, p, e)
        for direction, half in routes(kind, o, p, e):
            if half:
                view = half_of(kind, half, index)
                push(view, view, (kind, seen_from(direction, o, p, e), half), direction)
                continue
            view = gathered[kind].at[index]
            if direction == "c":
                recv = csem.at[0 if kind == "D" else 1]
            else:
                recv = rsem.at[slot((kind, seen_from(direction, o, p, e)))]
            pltpu.make_async_remote_copy(
                view, view, gsem.at[group_index[direction]], recv, device_id=devices[direction], device_id_type=MESH
            ).start()
            grouped[direction] = grouped.get(direction, 0) + 1

    def take(kind, o, p, e):
        index = block(o, p, e)
        if p == 0 and o == 2 and (e == 0 or kind == "U"):
            for half in "ab":
                arrived(half_of(kind, half, index), (kind, (o, p, e), half))
        else:
            arrived(gathered[kind].at[index], (kind, (o, p, e)))
        forward(kind, o, p, e)

    loads["tu"].wait()
    loads["td"].wait()
    push(tu_v.at[zo[2]], ru_a, "ru_a", "z+")
    push(td_v.at[zo[2]], rd_a, "rd_a", "z-")
    push(td_v.at[zo[1]], rd_m, "rd_m", "z+")
    push(tu_v.at[zo[3]], ru_p, "ru_p", "z-")

    on_low = t == 0

    def pick(low, high):
        return jnp.where(on_low, low, high)

    half = mu_v.shape[1] // 2
    loads["mu"].wait()
    loads["vu"].wait()
    m_other = pick(mu_v[:, half:], mu_v[:, :half])
    v_other = pick(vu_v[:, half:], vu_v[:, :half])
    cs[...] = (-0.05 * m_other - 0.175 * v_other).astype(BF16)
    push(cs, cr, "cr", "t")
    loads["tn"].wait()
    for direction, name in (("z+", "n3"), ("z-", "n1"), ("z2", "n2")):
        push(nb.at[z], nb.at[z], name, direction)

    loads["me"].wait()

    @pl.loop(0, 4)
    def _(k):
        mb[z * 4 + k] = m_v[k].astype(BF16)

    def send_master(up, down):
        push(mb.at[z * 4 + up], mb.at[z * 4 + up], ("m-", up), "z+")
        push(mb.at[z * 4 + down], mb.at[z * 4 + down], ("m+", down), "z-")

    def relay_master(up, down):
        from_minus, from_plus = mb.at[zo[3] * 4 + up], mb.at[zo[1] * 4 + down]
        arrived(from_minus, ("m-", up))
        push(from_minus, from_minus, ("m2", up), "z+")
        arrived(from_plus, ("m+", down))
        push(from_plus, from_plus, ("m2", down), "z-")

    arrived(ru_a, "ru_a")
    su[...] = (ru_a[...].astype(F32) + tu_v[zo[1]].astype(F32)).astype(BF16)
    push(su, ru_m, "ru_m", "z+")
    arrived(rd_a, "rd_a")
    sd[...] = (rd_a[...].astype(F32) + td_v[zo[3]].astype(F32)).astype(BF16)
    push(sd, rd_p, "rd_p", "z-")
    send_master(0, 2)

    loads["bt"].wait()
    high = bt_v[...].astype(BF16)
    bs[:64] = high
    bs[64:] = (bt_v[...] - high.astype(F32)).astype(BF16)
    loads["te"].wait()

    @pl.loop(0, 4)
    def _(j):
        both = nt_dot(bs[...], te_v[j])
        one = both[:64] + both[64:]
        pf[j] = one
        pp[j] = one.astype(BF16)

    for direction, o, name in (("z+", 1, "p3"), ("z-", 3, "p1"), ("z2", 2, "p2")):
        push(pp.at[zo[o]], pr.at[z], name, direction)

    loads["md"].wait()
    loads["vd"].wait()
    arrived(rd_m, "rd_m")
    arrived(rd_p, "rd_p")
    down_sum = rd_p[...].astype(F32) + rd_m[...].astype(F32) + td_v[z].astype(F32)
    stored, velocity = outer_step(md_v[...], vd_v[...], down_sum)
    RD[block(0, 0, 0)] = stored.astype(BF16)
    forward("D", 0, 0, 0)
    SD[...] = stored
    VD[...] = velocity

    arrived(ru_p, "ru_p")
    arrived(ru_m, "ru_m")
    arrived(cr, "cr")
    up_sum = ru_m[...].astype(F32) + ru_p[...].astype(F32) + tu_v[z].astype(F32)
    own, other = pick(up_sum[:8], up_sum[8:]), pick(up_sum[8:], up_sum[:8])
    m_own = pick(mu_v[:, :half], mu_v[:, half:])
    v_own = pick(vu_v[:, :half], vu_v[:, half:])
    own_new = outer_step(m_own, v_own, own)[0]
    other_new = 0.2625 * other + cr[...].astype(F32)
    RU[block(0, 0, 0)] = jnp.concatenate([pick(own_new, other_new), pick(other_new, own_new)], axis=0).astype(BF16)
    forward("U", 0, 0, 0)
    so[...] = own
    xs[...] = other.astype(BF16)
    push(xs, xr, "xr", "t")

    mq = jnp.zeros((64, 256), F32)
    loads["ve"].wait()
    for k in range(4):
        rows = m_v[k]
        low = (rows - rows.astype(BF16).astype(F32)).astype(BF16)
        both = nt_dot(bs[...], mb[z * 4 + k])
        ms[k] = both[:64] + both[64:] + nt_dot(bs[:64], low)

    def recast(o):
        w = wv[zo[o]].astype(F32).T

        for k in range(4):
            part = jnp.dot(w[k * 64 : (k + 1) * 64].astype(BF16), bs[:64], preferred_element_type=F32)
            if o == 0:
                new = m_v[k] - 0.7 * part
                SE[pl.ds(k * 64, 64)] = new
            else:
                new = mb[zo[o] * 4 + k].astype(F32) - 0.7 * part
            RE[zo[o] * 4 + k] = new.astype(BF16)

    def weights():
        for o in (1, 2, 3):
            arrived(pr.at[zo[o]], f"p{o}")
        total = pf[z] + pr[zo[1]].astype(F32) + pr[zo[2]].astype(F32) + pr[zo[3]].astype(F32)
        coefficient = jnp.concatenate([ms[k] for k in range(4)], axis=1) - 0.25 * total
        new = 0.5 * ve_v[...] + coefficient
        VE[...] = new
        wv[z] = (coefficient + 0.5 * new).astype(BF16)
        for direction, name in (("z+", "w3"), ("z-", "w1"), ("z2", "w2")):
            push(wv.at[z], wv.at[z], name, direction)
        recast(0)

    def local_steps():
        arrived(xr, "xr")
        for h in range(2):
            columns = pl.ds(h * half, half)
            mine = jnp.where(t == h, so[...], xr[...].astype(F32))
            stored, velocity = outer_step(mu_v[:, columns], vu_v[:, columns], mine)
            SU[:, columns] = stored
            VU[:, columns] = velocity
        for o in (1, 2, 3):
            arrived(nb.at[zo[o]], f"n{o}")
        loads["mn"].wait()
        loads["vn"].wait()
        total = nb[0].astype(F32) + nb[1].astype(F32) + nb[2].astype(F32) + nb[3].astype(F32)
        stored, velocity = outer_step(mn_v[...], vn_v[...], total)
        SN[...] = stored
        VN[...] = velocity
        RN[...] = stored.astype(BF16)

    def near_rows():
        for o, side in ((3, "m-"), (1, "m+")):
            for k in {"m-": (2, 3), "m+": (0, 1)}[side]:
                arrived(mb.at[zo[o] * 4 + k], (side, k))
            arrived(wv.at[zo[o]], f"w{o}")
            recast(o)

    def far_rows():
        for k in range(4):
            arrived(mb.at[zo[2] * 4 + k], ("m2", k))
        arrived(wv.at[zo[2]], "w2")
        recast(2)

    extra = {
        "m1": lambda: send_master(1, 3),
        "m2": lambda: send_master(2, 0),
        "m3": lambda: send_master(3, 1),
        "r0": lambda: relay_master(0, 2),
        "r1": lambda: relay_master(1, 3),
        "pw": weights,
        "x": local_steps,
        "e0": near_rows,
        "e1": far_rows,
    }
    for name in ORDER:
        if name in extra:
            extra[name]()
        else:
            take(name[0], int(name[1]), int(name[2]), int(name[3]))

    for i, ref in enumerate((RD, RU)):
        view = ref.at[pl.ds(0, 32)]
        pltpu.make_async_remote_copy(
            view, view, ssem.at[0], csem.at[i], device_id=devices["c"], device_id_type=MESH
        ).wait_recv()
    for copy in single:
        copy.wait_send()
    for direction, n in grouped.items():
        view = RD.at[pl.ds(0, n)]
        pltpu.make_async_remote_copy(
            view, view, gsem.at[group_index[direction]], rsem.at[0], device_id=devices["c"], device_id_type=MESH
        ).wait_send()


def flush(*refs):
    sources, targets, sem = refs[:12], refs[12:24], refs[24]
    copies = []
    for source, target in zip(sources, targets):
        pieces = 4 if source.shape[0] in (64, 16) and len(source.shape) == 3 else 1
        rows = source.shape[0] // pieces
        for i in range(pieces):
            part = pl.ds(i * rows, rows)
            copies.append(pltpu.make_async_copy(source.at[part], target.at[part], sem.at[len(copies)]))
            copies[-1].start()
    for copy in copies:
        copy.wait()


def body(
    trained_up,
    trained_down,
    trained_embed,
    trained_norm,
    master_up,
    moment_up,
    master_down,
    moment_down,
    master_embed,
    moment_embed,
    master_norm,
    moment_norm,
    embed_basis,
):
    operands = (
        trained_up.reshape(4, 16, 16, 2048),
        trained_down.reshape(4, 16, 32, 1024),
        trained_embed.reshape(4, 256, 1024),
        trained_norm[0],
        master_up,
        moment_up,
        master_down[0],
        moment_down[0],
        master_embed.reshape(4, 64, 1024),
        moment_embed[0].T,
        master_norm,
        moment_norm,
        embed_basis.T,
    )
    shapes = (
        ((64, 16, 2048), BF16),
        ((64, 32, 1024), BF16),
        ((16, 64, 1024), BF16),
        ((2, 1024), BF16),
        ((8, 4096), F32),
        ((8, 4096), F32),
        ((32, 1024), F32),
        ((32, 1024), F32),
        ((256, 1024), F32),
        ((64, 256), F32),
        ((2, 1024), F32),
        ((2, 1024), F32),
    )
    hbm = pl.BlockSpec(memory_space=pltpu.HBM)
    vmem = pl.BlockSpec(memory_space=pltpu.VMEM)
    new = pl.pallas_call(
        exchange,
        out_shape=tuple(pltpu.VMEM(shape, dtype) for shape, dtype in shapes),
        in_specs=[hbm] * 13,
        out_specs=[vmem] * 12,
        scratch_shapes=[
            pltpu.VMEM((4, 16, 2048), BF16),
            pltpu.VMEM((4, 32, 1024), BF16),
            pltpu.VMEM((4, 256, 1024), BF16),
            pltpu.VMEM((4, 2, 1024), BF16),
            pltpu.VMEM((8, 4096), F32),
            pltpu.VMEM((8, 4096), F32),
            pltpu.VMEM((32, 1024), F32),
            pltpu.VMEM((32, 1024), F32),
            pltpu.VMEM((4, 64, 1024), F32),
            pltpu.VMEM((64, 256), F32),
            pltpu.VMEM((2, 1024), F32),
            pltpu.VMEM((2, 1024), F32),
            pltpu.VMEM((64, 1024), F32),
            pltpu.VMEM((16, 2048), BF16),
            pltpu.VMEM((16, 2048), BF16),
            pltpu.VMEM((16, 2048), BF16),
            pltpu.VMEM((32, 1024), BF16),
            pltpu.VMEM((32, 1024), BF16),
            pltpu.VMEM((32, 1024), BF16),
            pltpu.VMEM((16, 2048), BF16),
            pltpu.VMEM((32, 1024), BF16),
            pltpu.VMEM((8, 2048), BF16),
            pltpu.VMEM((8, 2048), BF16),
            pltpu.VMEM((8, 2048), BF16),
            pltpu.VMEM((8, 2048), BF16),
            pltpu.VMEM((8, 2048), F32),
            pltpu.VMEM((128, 1024), BF16),
            pltpu.VMEM((16, 64, 1024), BF16),
            pltpu.VMEM((4, 64, 256), F32),
            pltpu.VMEM((4, 64, 256), BF16),
            pltpu.VMEM((4, 64, 256), BF16),
            pltpu.VMEM((4, 64, 256), BF16),
            pltpu.VMEM((4, 64, 64), F32),
            pltpu.SemaphoreType.DMA((13,)),
            pltpu.SemaphoreType.DMA((N_SEND,)),
            pltpu.SemaphoreType.DMA((6,)),
            pltpu.SemaphoreType.DMA((N_RECV,)),
            pltpu.SemaphoreType.DMA((2,)),
        ],
        compiler_params=pltpu.CompilerParams(
            collective_id=0, has_side_effects=True, vmem_limit_bytes=24 << 20
        ),
        name="exchange",
    )(*[pltpu.with_memory_space_constraint(a, pltpu.HBM) for a in operands])
    new = [pltpu.with_memory_space_constraint(a, pltpu.VMEM) for a in new]
    out = pl.pallas_call(
        flush,
        out_shape=tuple(jax.ShapeDtypeStruct(shape, dtype) for shape, dtype in shapes),
        in_specs=[vmem] * 12,
        out_specs=[hbm] * 12,
        scratch_shapes=[pltpu.SemaphoreType.DMA((21,))],
        compiler_params=pltpu.CompilerParams(vmem_limit_bytes=1 << 20),
        name="flush",
    )(*new)
    return (
        out[0].reshape(1024, 2048),
        out[1].reshape(2048, 1024),
        out[2].reshape(1024, 1024),
        out[3],
        out[4],
        out[5],
        out[6][None],
        out[7][None],
        out[8][None],
        out[9].T[None],
        out[10],
        out[11],
    )


def solution(mesh):
    in_specs = (
        P("replica", None, "tensor"),
        P("replica", "tensor", None),
        P("replica", ("shard", "tensor"), None),
        P("replica", None, None),
        P(("replica", "shard", "tensor"), None),
        P(("replica", "shard", "tensor"), None),
        P("tensor", ("replica", "shard"), None),
        P("tensor", ("replica", "shard"), None),
        P(("shard", "tensor"), "replica", None),
        P(("shard", "tensor"), "replica", None),
        P(),
        P(),
        P(),
    )
    out_specs = (
        P(None, "tensor"),
        P("tensor", None),
        P(("shard", "tensor"), None),
        P(),
        P(("replica", "shard", "tensor"), None),
        P(("replica", "shard", "tensor"), None),
        P("tensor", ("replica", "shard"), None),
        P("tensor", ("replica", "shard"), None),
        P(("shard", "tensor"), "replica", None),
        P(("shard", "tensor"), "replica", None),
        P(),
        P(),
    )
    return jax.shard_map(body, mesh=mesh, in_specs=in_specs, out_specs=out_specs, check_vma=False)
```

time: 377 us -> 54.4 us (0.14)
  waiting for transfers between devices: 316 us -> 0 us
  Pallas kernels: 0 us -> 53.6 us
  blocking collectives: 23 us -> 0 us
  between operations: 14.3 us -> 0.66 us
  local copies, waits for them, and re-layouts: 13.4 us -> 0 us
  other arithmetic: 5.09 us -> 0 us
  matrix products: 4.38 us -> 0 us
    all_gather x3 -> x0, waiting for transfers between devices: 240 us -> none  [the longest x1 108 us: body(): lax.all_gather(up_piece, ('replica', 'shard'), axis=0, tiled=True)]
    pallas_call x0 -> x2, Pallas kernels: none -> 53.6 us  [the longest x1 49 us: body(): pl.pallas_call(exchange, out_shape=tuple((pltpu.VMEM(shape, dtype) for sh...]
    unnamed x7 -> x0, waiting for transfers between devices: 38.1 us -> none
    reduce_scatter x2 -> x0, waiting for transfers between devices: 37.9 us -> none  [the longest x1 32.1 us: body(): lax.psum_scatter(embed_terms.astype(jnp.bfloat16), 'replica', scatter_dim...]
    all_to_all x2 -> x0, blocking collectives: 16.1 us -> none  [the longest x1 8.59 us: body(): lax.all_to_all(up_summed, 'tensor', split_axis=1, concat_axis=3, tiled=True)]
    unnamed x30 -> x0, local copies, waits for them, and re-layouts: 10 us -> none
    psum x1 -> x0, blocking collectives: 6.93 us -> none  [body(): norm_summed = lax.psum(trained_norm[0].astype(jnp.float32), 'replica')]
    convert_element_type x5 -> x0, other arithmetic: 4.45 us -> none  [the longest x1 1.6 us: body(): down_piece = stored_down[0].astype(jnp.bfloat16)]
  transfers between devices with their start and end apart: 6 -> 0, of which waited for: 6 -> 0; matrix products, arithmetic and copies ran while one was open for 4% -> 0% of each run, Pallas kernels for 0% -> 0%
where the time goes in v1:
time: 54.4 us; the launch traced here: 54.3 us
  Pallas kernels  53.6 us (99%)
  between operations  0.66 us (1%)
    pallas_call x1, Pallas kernels, body(): pl.pallas_call(exchange, out_shape=tuple((pltpu.VMEM(shape, dtype) for sh...  49 us
    pallas_call x1, Pallas kernels, body(): pl.pallas_call(flush, out_shape=tuple((jax.ShapeDtypeStruct(shape, dtype)...  4.61 us

profile of v1, /device:TPU:1, one launch (start us, length us, event | category | flops | bytes accessed | tf_op | source)
XLA Modules:
  0.0 54.3 jit_solution(14603737155274590623)
XLA Ops:
  0.6 49.0 %exchange.1 = (bf16[64,16,2048]{2,1,0:T(8,128)(2,1)S(1)}, bf16[64,32,1024]{2,1,0:T(8,128)(2,1)S(1)}, bf16[16,64,1024]{2,1,0:T(8,128)(2,1)S(1)}, bf16[2,1024]{1,0...) custom-call(bf16[4,16,16,2048]{3,2,1,0:T(8,128)(2,1)} %bitcast.20, ...), custom_call_target="tpu_custom_call" | custom-call | tf_op jit(solution)/shard_map/exchange/pallas_call | solution.py:422
  49.6 4.6 %flush.1 = (bf16[64,16,2048]{2,1,0:T(8,128)(2,1)}, bf16[64,32,1024]{2,1,0:T(8,128)(2,1)}, bf16[16,64,1024]{2,1,0:T(8,128)(2,1)}, bf16[2,1024]{1,0:T(2,128)(2,1)}...) custom-call(bf16[64,16,2048]{2,1,0:T(8,128)(2,1)S(1)} %get-tuple-ele, ...), custom_call_target="tpu_custom_call" | custom-call | tf_op jit(solution)/shard_map/flush/pallas_call | solution.py:473

commit v2 on v1

--- a/solution.py
+++ b/solution.py
@@ -1,3 +1,5 @@
+import heapq
+
 import jax
 import jax.numpy as jnp
 from jax import lax
@@ -8,34 +10,19 @@
 MESH = pl.DeviceIdType.MESH
 F32, BF16 = jnp.float32, jnp.bfloat16
 
-ORDER = [
-    "D030", "D010", "D001", "D300", "D100", "U001", "U030", "U010", "U300", "U100",
-    "m1", "pw",
-    "D020", "D031", "D310", "D011", "D330", "D110", "D200", "D301", "D130", "r0",
-    "U011", "D101", "U031", "U310", "U020", "D021", "U110", "U301", "U101",
-    "m2", "m3", "U330", "D311", "U200", "D320", "x", "U130", "D331", "D120", "D111", "D230", "D210",
-    "D201", "U331", "U021", "r1", "D131", "U131", "U201", "e0", "U320", "U230", "D321", "U120", "D121", "D220",
-    "U311", "D231", "e1", "U321", "U111", "D211", "U121", "U210", "U220", "D221", "U211", "U231", "U221",
-]
-
-
-def routes(kind, o, p, e):
-    every_y = [("y+", ""), ("y-", "")]
+OWN = (0, 0, 0)
+
+
+def routes(kind, h, o, p, e):
+    z_part = {0: ["z+", "z-"], 3: ["z+"] * (h == 0), 1: ["z-"] * (h == 1), 2: []}[o]
+    y_part = {0: ["y+", "y-"], 3: ["y+"] * (h == 0), 1: ["y-"] * (h == 1), 2: []}[p]
     if kind == "D":
-        if p == 0 and e == 0:
-            z_part = {0: [("z+", ""), ("z-", "")], 3: [("z+", "a")], 1: [("z-", "b")], 2: []}[o]
-            return z_part + every_y + [("x", ""), ("c", "")]
-        if e == 0:
-            relay = [("y+", "")] if p == 3 and o % 2 == 0 else [("y-", "")] if p == 1 and o % 2 == 1 else []
-            return relay + [("x", ""), ("c", "")]
-        return [("c", "")]
-    if p == 0:
-        x_part = [("x", "")] if o == 0 and e == 0 else []
-        z_part = {0: [("z+", ""), ("z-", "")], 3: [("z+", "a")], 1: [("z-", "b")], 2: []}[o]
-        return x_part + z_part + every_y + [("c", "")]
-    odd = (o + e) % 2
-    relay = [("y+", "")] if p == 3 and not odd else [("y-", "")] if p == 1 and odd else []
-    return relay + [("c", "")]
+        if e:
+            return []
+        return (z_part if p == 0 else []) + y_part + ["x"]
+    if p:
+        return y_part
+    return (["x"] if o == 0 and e == 0 else []) + z_part + y_part
 
 
 def seen_from(direction, o, p, e):
@@ -47,9 +34,74 @@
         return o, (p + 3) % 4, e
     if direction == "y-":
         return o, (p + 1) % 4, e
-    if direction == "x":
-        return o, p, 1 - e
-    return o, p, e
+    return o, p, 1 - e
+
+
+def rank(piece, direction):
+    kind, h, o, p, e = piece
+    if kind == "D":
+        return 1 if direction == "x" else 0
+    if direction[0] == "y":
+        return 2 if p == 0 else 3
+    return 0 if direction == "x" else 1
+
+
+FIRST = 1
+NEAR, FAR = 24.4, 19.0
+HOP, PIECE, LEAD = 2.2, 0.705, 2.1
+READY = {("D", 0): 0.0, ("D", 1): 0.5, ("U", 0): 0.8, ("U", 1): 1.2}
+EXTRA = [(12.0, "weights"), (9.0, "swap"), (17.0, "local"), (NEAR, "near"), (FAR, "far")]
+
+
+def plan():
+    links = ["z+", "z-", "y+", "y-", "x"]
+    free = dict.fromkeys(links, 0.0)
+    waiting = {link: [] for link in links}
+    events, steps = [], []
+
+    def at(when, what):
+        at.count += 1
+        heapq.heappush(events, (when, at.count, what))
+
+    def offer(link, order, what):
+        at.count += 1
+        heapq.heappush(waiting[link], (order, at.count, what))
+
+    at.count = 0
+    for (kind, h), when in READY.items():
+        at(when, ("take", (kind, h) + OWN))
+    for when, name in EXTRA:
+        at(when, ("extra", name))
+    free["z+"] = free["z-"] = 0.5
+    for link, first in (("z+", 0), ("z-", 4)):
+        for i in range(FIRST, 8):
+            offer(link, 3 if i < 4 else 5, ("own", (first + i) % 8))
+    for i in range(FIRST):
+        at(HOP, ("relay", "z+", i))
+        at(HOP, ("relay", "z-", 4 + i))
+    while events:
+        now, _, what = heapq.heappop(events)
+        if what[0] == "take":
+            steps.append(what)
+            for link in routes(*what[1]):
+                offer(link, rank(what[1], link), ("piece", what[1]))
+        elif what[0] == "relay":
+            offer(what[1], 4, ("relay", what[2]))
+        elif what[0] == "extra":
+            steps.append(what)
+        for link in links:
+            while waiting[link] and free[link] <= now + LEAD:
+                _, _, (sort, which) = heapq.heappop(waiting[link])
+                begin = max(free[link], now)
+                free[link] = begin + PIECE * (1 if sort == "piece" else 2)
+                steps.append((sort, which, link))
+                landed = free[link] + HOP
+                if sort == "piece":
+                    at(landed, ("take", which[:2] + seen_from(link, *which[2:])))
+                elif sort == "own" and (which < 4) == (link == "z+"):
+                    at(landed, ("relay", link, which))
+                at(free[link] - LEAD, ("turn",))
+    return steps
 
 
 def outer_step(master, moment, summed):
@@ -69,15 +121,15 @@
     return SLOTS.setdefault(key, len(SLOTS))
 
 
-N_RECV = 104
-N_SEND = 56
+N_RECV = 176
+N_SEND = 72
 
 
 def exchange(
     tu, td, te, tn, mu, vu, md, vd, me, ve, mn, vn, bt,
     RU, RD, RE, RN, SU, VU, SD, VD, SE, VE, SN, VN,
     tu_v, td_v, te_v, nb, mu_v, vu_v, md_v, vd_v, m_v, ve_v, mn_v, vn_v, bt_v,
-    ru_a, ru_m, ru_p, rd_a, rd_m, rd_p, su, sd, cs, cr, xs, xr, so,
+    ru_a, ru_m, ru_p, rd_a, rd_m, rd_p, su, sd, cs, cr, xs, xr, so, tot,
     bs, mb, pf, pp, pr, wv, ms,
     lsem, ssem, gsem, rsem, csem,
 ):
@@ -145,42 +197,32 @@
     gathered = {"D": RD, "U": RU}
     half_rows = {"D": 16, "U": 8}
 
-    def half_of(kind, which, index):
-        n = half_rows[kind]
-        return gathered[kind].at[index, pl.ds(0 if which == "a" else n, n)]
-
-    def forward(kind, o, p, e):
-        index = block(o, p, e)
-        for direction, half in routes(kind, o, p, e):
-            if half:
-                view = half_of(kind, half, index)
-                push(view, view, (kind, seen_from(direction, o, p, e), half), direction)
-                continue
-            view = gathered[kind].at[index]
-            if direction == "c":
-                recv = csem.at[0 if kind == "D" else 1]
-            else:
-                recv = rsem.at[slot((kind, seen_from(direction, o, p, e)))]
-            pltpu.make_async_remote_copy(
-                view, view, gsem.at[group_index[direction]], recv, device_id=devices[direction], device_id_type=MESH
-            ).start()
-            grouped[direction] = grouped.get(direction, 0) + 1
-
-    def take(kind, o, p, e):
-        index = block(o, p, e)
-        if p == 0 and o == 2 and (e == 0 or kind == "U"):
-            for half in "ab":
-                arrived(half_of(kind, half, index), (kind, (o, p, e), half))
+    def rows(kind, h):
+        return pl.ds(h * half_rows[kind], half_rows[kind])
+
+    def view(kind, h, o, p, e):
+        return gathered[kind].at[block(o, p, e), rows(kind, h)]
+
+    def forward(piece, direction):
+        kind, h = piece[:2]
+        ref = view(*piece)
+        if direction == "c":
+            recv = csem.at[0 if kind == "D" else 1]
         else:
-            arrived(gathered[kind].at[index], (kind, (o, p, e)))
-        forward(kind, o, p, e)
+            recv = rsem.at[slot((kind, h, seen_from(direction, *piece[2:])))]
+        pltpu.make_async_remote_copy(
+            ref, ref, gsem.at[group_index[direction]], recv, device_id=devices[direction], device_id_type=MESH
+        ).start()
+        grouped[direction] = grouped.get(direction, 0) + 1
 
     loads["tu"].wait()
     loads["td"].wait()
-    push(tu_v.at[zo[2]], ru_a, "ru_a", "z+")
-    push(td_v.at[zo[2]], rd_a, "rd_a", "z-")
-    push(td_v.at[zo[1]], rd_m, "rd_m", "z+")
-    push(tu_v.at[zo[3]], ru_p, "ru_p", "z-")
+    for h in range(2):
+        push(td_v.at[zo[2], rows("D", h)], rd_a.at[rows("D", h)], ("da", h), "z-")
+        push(tu_v.at[zo[2], rows("U", h)], ru_a.at[rows("U", h)], ("ua", h), "z+")
+    for h in range(2):
+        push(td_v.at[zo[1], rows("D", h)], rd_m.at[rows("D", h)], ("dm", h), "z+")
+        push(tu_v.at[zo[3], rows("U", h)], ru_p.at[rows("U", h)], ("up", h), "z-")
 
     on_low = t == 0
 
@@ -198,31 +240,6 @@
     for direction, name in (("z+", "n3"), ("z-", "n1"), ("z2", "n2")):
         push(nb.at[z], nb.at[z], name, direction)
 
-    loads["me"].wait()
-
-    @pl.loop(0, 4)
-    def _(k):
-        mb[z * 4 + k] = m_v[k].astype(BF16)
-
-    def send_master(up, down):
-        push(mb.at[z * 4 + up], mb.at[z * 4 + up], ("m-", up), "z+")
-        push(mb.at[z * 4 + down], mb.at[z * 4 + down], ("m+", down), "z-")
-
-    def relay_master(up, down):
-        from_minus, from_plus = mb.at[zo[3] * 4 + up], mb.at[zo[1] * 4 + down]
-        arrived(from_minus, ("m-", up))
-        push(from_minus, from_minus, ("m2", up), "z+")
-        arrived(from_plus, ("m+", down))
-        push(from_plus, from_plus, ("m2", down), "z-")
-
-    arrived(ru_a, "ru_a")
-    su[...] = (ru_a[...].astype(F32) + tu_v[zo[1]].astype(F32)).astype(BF16)
-    push(su, ru_m, "ru_m", "z+")
-    arrived(rd_a, "rd_a")
-    sd[...] = (rd_a[...].astype(F32) + td_v[zo[3]].astype(F32)).astype(BF16)
-    push(sd, rd_p, "rd_p", "z-")
-    send_master(0, 2)
-
     loads["bt"].wait()
     high = bt_v[...].astype(BF16)
     bs[:64] = high
@@ -236,42 +253,70 @@
         pf[j] = one
         pp[j] = one.astype(BF16)
 
+    for h in range(2):
+        d, u = rows("D", h), rows("U", h)
+        arrived(rd_a.at[d], ("da", h))
+        sd[d] = (rd_a[d].astype(F32) + td_v[zo[3], d].astype(F32)).astype(BF16)
+        push(sd.at[d], rd_p.at[d], ("dp", h), "z-")
+        arrived(ru_a.at[u], ("ua", h))
+        su[u] = (ru_a[u].astype(F32) + tu_v[zo[1], u].astype(F32)).astype(BF16)
+        push(su.at[u], ru_m.at[u], ("um", h), "z+")
+
+    loads["me"].wait()
+
+    @pl.loop(0, 4)
+    def _(k):
+        mb[z * 4 + k] = m_v[k].astype(BF16)
+
+    def master(o, j):
+        return mb.at[zo[o] * 4 + j // 2, pl.ds(j % 2 * 32, 32)]
+
+    def send_master(j, direction):
+        push(master(0, j), master(0, j), ({"z+": "m-", "z-": "m+"}[direction], j), direction)
+
+    def relay_master(j, direction):
+        side, o = ("m-", 3) if direction == "z+" else ("m+", 1)
+        arrived(master(o, j), (side, j))
+        push(master(o, j), master(o, j), ("m2", j), direction)
+
+    for i in range(FIRST):
+        send_master(i, "z+")
+        send_master(4 + i, "z-")
     for direction, o, name in (("z+", 1, "p3"), ("z-", 3, "p1"), ("z2", 2, "p2")):
         push(pp.at[zo[o]], pr.at[z], name, direction)
 
     loads["md"].wait()
     loads["vd"].wait()
-    arrived(rd_m, "rd_m")
-    arrived(rd_p, "rd_p")
-    down_sum = rd_p[...].astype(F32) + rd_m[...].astype(F32) + td_v[z].astype(F32)
-    stored, velocity = outer_step(md_v[...], vd_v[...], down_sum)
-    RD[block(0, 0, 0)] = stored.astype(BF16)
-    forward("D", 0, 0, 0)
-    SD[...] = stored
-    VD[...] = velocity
-
-    arrived(ru_p, "ru_p")
-    arrived(ru_m, "ru_m")
-    arrived(cr, "cr")
-    up_sum = ru_m[...].astype(F32) + ru_p[...].astype(F32) + tu_v[z].astype(F32)
-    own, other = pick(up_sum[:8], up_sum[8:]), pick(up_sum[8:], up_sum[:8])
-    m_own = pick(mu_v[:, :half], mu_v[:, half:])
-    v_own = pick(vu_v[:, :half], vu_v[:, half:])
-    own_new = outer_step(m_own, v_own, own)[0]
-    other_new = 0.2625 * other + cr[...].astype(F32)
-    RU[block(0, 0, 0)] = jnp.concatenate([pick(own_new, other_new), pick(other_new, own_new)], axis=0).astype(BF16)
-    forward("U", 0, 0, 0)
-    so[...] = own
-    xs[...] = other.astype(BF16)
-    push(xs, xr, "xr", "t")
-
-    mq = jnp.zeros((64, 256), F32)
-    loads["ve"].wait()
-    for k in range(4):
-        rows = m_v[k]
-        low = (rows - rows.astype(BF16).astype(F32)).astype(BF16)
-        both = nt_dot(bs[...], mb[z * 4 + k])
-        ms[k] = both[:64] + both[64:] + nt_dot(bs[:64], low)
+
+    def own_down(h):
+        d = rows("D", h)
+        arrived(rd_m.at[d], ("dm", h))
+        arrived(rd_p.at[d], ("dp", h))
+        total = rd_p[d].astype(F32) + rd_m[d].astype(F32) + td_v[z, d].astype(F32)
+        stored, velocity = outer_step(md_v[d], vd_v[d], total)
+        RD[block(*OWN), d] = stored.astype(BF16)
+        SD[d] = stored
+        VD[d] = velocity
+
+    def own_up(h):
+        u = rows("U", h)
+        arrived(ru_p.at[u], ("up", h))
+        arrived(ru_m.at[u], ("um", h))
+        if h == 0:
+            arrived(cr, "cr")
+        total = ru_m[u].astype(F32) + ru_p[u].astype(F32) + tu_v[z, u].astype(F32)
+        m_own = pick(mu_v[:, :half], mu_v[:, half:])
+        v_own = pick(vu_v[:, :half], vu_v[:, half:])
+        mine = outer_step(m_own, v_own, total)[0]
+        other = 0.2625 * total + cr[...].astype(F32)
+        RU[block(*OWN), u] = jnp.where(t == h, mine, other).astype(BF16)
+        tot[u] = total
+
+    def swap():
+        own, other = pick(tot[:8], tot[8:]), pick(tot[8:], tot[:8])
+        so[...] = own
+        xs[...] = other.astype(BF16)
+        push(xs, xr, "xr", "t")
 
     def recast(o):
         w = wv[zo[o]].astype(F32).T
@@ -286,6 +331,11 @@
             RE[zo[o] * 4 + k] = new.astype(BF16)
 
     def weights():
+        loads["ve"].wait()
+        for k in range(4):
+            low = (m_v[k] - m_v[k].astype(BF16).astype(F32)).astype(BF16)
+            both = nt_dot(bs[...], mb[z * 4 + k])
+            ms[k] = both[:64] + both[64:] + nt_dot(bs[:64], low)
         for o in (1, 2, 3):
             arrived(pr.at[zo[o]], f"p{o}")
         total = pf[z] + pr[zo[1]].astype(F32) + pr[zo[2]].astype(F32) + pr[zo[3]].astype(F32)
@@ -317,45 +367,48 @@
 
     def near_rows():
         for o, side in ((3, "m-"), (1, "m+")):
-            for k in {"m-": (2, 3), "m+": (0, 1)}[side]:
-                arrived(mb.at[zo[o] * 4 + k], (side, k))
+            for j in {"m-": (4, 5, 6, 7), "m+": (0, 1, 2, 3)}[side]:
+                arrived(master(o, j), (side, j))
             arrived(wv.at[zo[o]], f"w{o}")
             recast(o)
 
     def far_rows():
-        for k in range(4):
-            arrived(mb.at[zo[2] * 4 + k], ("m2", k))
+        for j in range(8):
+            arrived(master(2, j), ("m2", j))
         arrived(wv.at[zo[2]], "w2")
         recast(2)
 
-    extra = {
-        "m1": lambda: send_master(1, 3),
-        "m2": lambda: send_master(2, 0),
-        "m3": lambda: send_master(3, 1),
-        "r0": lambda: relay_master(0, 2),
-        "r1": lambda: relay_master(1, 3),
-        "pw": weights,
-        "x": local_steps,
-        "e0": near_rows,
-        "e1": far_rows,
-    }
-    for name in ORDER:
-        if name in extra:
-            extra[name]()
+    def take(kind, h, o, p, e):
+        if (o, p, e) == OWN:
+            {"D": own_down, "U": own_up}[kind](h)
         else:
-            take(name[0], int(name[1]), int(name[2]), int(name[3]))
+            arrived(view(kind, h, o, p, e), (kind, h, (o, p, e)))
+        forward((kind, h, o, p, e), "c")
+
+    extra = {"weights": weights, "swap": swap, "local": local_steps, "near": near_rows, "far": far_rows}
+    for step in plan():
+        if step[0] == "take":
+            take(*step[1])
+        elif step[0] == "piece":
+            forward(step[1], step[2])
+        elif step[0] == "own":
+            send_master(step[1], step[2])
+        elif step[0] == "relay":
+            relay_master(step[1], step[2])
+        else:
+            extra[step[1]]()
 
     for i, ref in enumerate((RD, RU)):
-        view = ref.at[pl.ds(0, 32)]
+        landed = ref.at[pl.ds(0, 32)]
         pltpu.make_async_remote_copy(
-            view, view, ssem.at[0], csem.at[i], device_id=devices["c"], device_id_type=MESH
+            landed, landed, ssem.at[0], csem.at[i], device_id=devices["c"], device_id_type=MESH
         ).wait_recv()
     for copy in single:
         copy.wait_send()
     for direction, n in grouped.items():
-        view = RD.at[pl.ds(0, n)]
+        sent = RD.at[pl.ds(0, n // 2)] if n > 64 else RD.at[pl.ds(0, n), pl.ds(0, 16)]
         pltpu.make_async_remote_copy(
-            view, view, gsem.at[group_index[direction]], rsem.at[0], device_id=devices["c"], device_id_type=MESH
+            sent, sent, gsem.at[group_index[direction]], rsem.at[0], device_id=devices["c"], device_id_type=MESH
         ).wait_send()
 
 
@@ -451,6 +504,7 @@
             pltpu.VMEM((8, 2048), BF16),
             pltpu.VMEM((8, 2048), BF16),
             pltpu.VMEM((8, 2048), F32),
+            pltpu.VMEM((16, 2048), F32),
             pltpu.VMEM((128, 1024), BF16),
             pltpu.VMEM((16, 64, 1024), BF16),
             pltpu.VMEM((4, 64, 256), F32),

time: 54.4 us -> 50.7 us (0.932)
  Pallas kernels: 53.6 us -> 49.9 us
    pallas_call x1, Pallas kernels: 49 us -> 45.3 us  [body(): pl.pallas_call(exchange, out_shape=tuple((pltpu.VMEM(shape, dtype) for sh...]
where the time goes in v2:
time: 50.7 us; the launch traced here: 50.6 us
  Pallas kernels  49.9 us (98%)
  between operations  0.66 us (1%)
    pallas_call x1, Pallas kernels, body(): pl.pallas_call(exchange, out_shape=tuple((pltpu.VMEM(shape, dtype) for sh...  45.3 us
    pallas_call x1, Pallas kernels, body(): pl.pallas_call(flush, out_shape=tuple((jax.ShapeDtypeStruct(shape, dtype)...  4.61 us

profile of v2, /device:TPU:1, one launch (start us, length us, event | category | flops | bytes accessed | tf_op | source)
XLA Modules:
  0.0 50.6 jit_solution(10685576522549795836)
XLA Ops:
  0.6 45.3 %exchange.1 = (bf16[64,16,2048]{2,1,0:T(8,128)(2,1)S(1)}, bf16[64,32,1024]{2,1,0:T(8,128)(2,1)S(1)}, bf16[16,64,1024]{2,1,0:T(8,128)(2,1)S(1)}, bf16[2,1024]{1,0...) custom-call(bf16[4,16,16,2048]{3,2,1,0:T(8,128)(2,1)} %bitcast.20, ...), custom_call_target="tpu_custom_call" | custom-call | tf_op jit(solution)/shard_map/exchange/pallas_call | solution.py:475
  46.0 4.6 %flush.1 = (bf16[64,16,2048]{2,1,0:T(8,128)(2,1)}, bf16[64,32,1024]{2,1,0:T(8,128)(2,1)}, bf16[16,64,1024]{2,1,0:T(8,128)(2,1)}, bf16[2,1024]{1,0:T(2,128)(2,1)}...) custom-call(bf16[64,16,2048]{2,1,0:T(8,128)(2,1)S(1)} %get-tuple-ele, ...), custom_call_target="tpu_custom_call" | custom-call | tf_op jit(solution)/shard_map/flush/pallas_call | solution.py:527

commit v3 on v2

--- a/solution.py
+++ b/solution.py
@@ -47,10 +47,23 @@
 
 
 FIRST = 1
-NEAR, FAR = 24.4, 19.0
-HOP, PIECE, LEAD = 2.2, 0.705, 2.1
+HOP, PIECE, LEAD = 2.0, 0.705, 2.1
 READY = {("D", 0): 0.0, ("D", 1): 0.5, ("U", 0): 0.8, ("U", 1): 1.2}
-EXTRA = [(12.0, "weights"), (9.0, "swap"), (17.0, "local"), (NEAR, "near"), (FAR, "far")]
+EXTRA = [
+    *((5.0 + j, "project", j) for j in range(4)),
+    *((9.0 + 0.8 * k, "master", k) for k in range(4)),
+    (12.2, "swap"),
+    (13.0, "weights"),
+    (14.0, "recast", 0, 0),
+    (15.0, "recast", 0, 1),
+    (17.0, "local"),
+    (19.5, "recast", 2, 0),
+    (20.5, "recast", 2, 1),
+    (21.5, "recast", 3, 0),
+    (22.5, "recast", 1, 1),
+    (25.2, "recast", 3, 1),
+    (25.4, "recast", 1, 0),
+]
 
 
 def plan():
@@ -70,8 +83,8 @@
     at.count = 0
     for (kind, h), when in READY.items():
         at(when, ("take", (kind, h) + OWN))
-    for when, name in EXTRA:
-        at(when, ("extra", name))
+    for when, *call in EXTRA:
+        at(when, ("extra", *call))
     free["z+"] = free["z-"] = 0.5
     for link, first in (("z+", 0), ("z-", 4)):
         for i in range(FIRST, 8):
@@ -240,19 +253,6 @@
     for direction, name in (("z+", "n3"), ("z-", "n1"), ("z2", "n2")):
         push(nb.at[z], nb.at[z], name, direction)
 
-    loads["bt"].wait()
-    high = bt_v[...].astype(BF16)
-    bs[:64] = high
-    bs[64:] = (bt_v[...] - high.astype(F32)).astype(BF16)
-    loads["te"].wait()
-
-    @pl.loop(0, 4)
-    def _(j):
-        both = nt_dot(bs[...], te_v[j])
-        one = both[:64] + both[64:]
-        pf[j] = one
-        pp[j] = one.astype(BF16)
-
     for h in range(2):
         d, u = rows("D", h), rows("U", h)
         arrived(rd_a.at[d], ("da", h))
@@ -282,9 +282,6 @@
     for i in range(FIRST):
         send_master(i, "z+")
         send_master(4 + i, "z-")
-    for direction, o, name in (("z+", 1, "p3"), ("z-", 3, "p1"), ("z2", 2, "p2")):
-        push(pp.at[zo[o]], pr.at[z], name, direction)
-
     loads["md"].wait()
     loads["vd"].wait()
 
@@ -318,24 +315,28 @@
         xs[...] = other.astype(BF16)
         push(xs, xr, "xr", "t")
 
-    def recast(o):
-        w = wv[zo[o]].astype(F32).T
-
-        for k in range(4):
-            part = jnp.dot(w[k * 64 : (k + 1) * 64].astype(BF16), bs[:64], preferred_element_type=F32)
-            if o == 0:
-                new = m_v[k] - 0.7 * part
-                SE[pl.ds(k * 64, 64)] = new
-            else:
-                new = mb[zo[o] * 4 + k].astype(F32) - 0.7 * part
-            RE[zo[o] * 4 + k] = new.astype(BF16)
+    def project(j):
+        if j == 0:
+            loads["bt"].wait()
+            high = bt_v[...].astype(BF16)
+            bs[:64] = high
+            bs[64:] = (bt_v[...] - high.astype(F32)).astype(BF16)
+            loads["te"].wait()
+        both = nt_dot(bs[...], te_v[j])
+        one = both[:64] + both[64:]
+        pf[j] = one
+        pp[j] = one.astype(BF16)
+        if j == 3:
+            for direction, o, name in (("z+", 1, "p3"), ("z-", 3, "p1"), ("z2", 2, "p2")):
+                push(pp.at[zo[o]], pr.at[z], name, direction)
+
+    def project_master(k):
+        low = (m_v[k] - m_v[k].astype(BF16).astype(F32)).astype(BF16)
+        both = nt_dot(bs[...], mb[z * 4 + k])
+        ms[k] = both[:64] + both[64:] + nt_dot(bs[:64], low)
 
     def weights():
         loads["ve"].wait()
-        for k in range(4):
-            low = (m_v[k] - m_v[k].astype(BF16).astype(F32)).astype(BF16)
-            both = nt_dot(bs[...], mb[z * 4 + k])
-            ms[k] = both[:64] + both[64:] + nt_dot(bs[:64], low)
         for o in (1, 2, 3):
             arrived(pr.at[zo[o]], f"p{o}")
         total = pf[z] + pr[zo[1]].astype(F32) + pr[zo[2]].astype(F32) + pr[zo[3]].astype(F32)
@@ -345,7 +346,30 @@
         wv[z] = (coefficient + 0.5 * new).astype(BF16)
         for direction, name in (("z+", "w3"), ("z-", "w1"), ("z2", "w2")):
             push(wv.at[z], wv.at[z], name, direction)
-        recast(0)
+
+    seen = set()
+
+    def recast(o, q):
+        if o and o not in seen:
+            seen.add(o)
+            arrived(wv.at[zo[o]], f"w{o}")
+        for j in range(4 * q, 4 * q + 4):
+            if o == 2:
+                arrived(master(2, j), ("m2", j))
+            elif o == 3 and q == 1:
+                arrived(master(3, j), ("m-", j))
+            elif o == 1 and q == 0:
+                arrived(master(1, j), ("m+", j))
+        w = wv[zo[o], :, q * 128 : (q + 1) * 128].astype(F32).T
+        for i in range(2):
+            k = 2 * q + i
+            part = jnp.dot(w[i * 64 : (i + 1) * 64].astype(BF16), bs[:64], preferred_element_type=F32)
+            if o == 0:
+                new = m_v[k] - 0.7 * part
+                SE[pl.ds(k * 64, 64)] = new
+            else:
+                new = mb[zo[o] * 4 + k].astype(F32) - 0.7 * part
+            RE[zo[o] * 4 + k] = new.astype(BF16)
 
     def local_steps():
         arrived(xr, "xr")
@@ -365,19 +389,6 @@
         VN[...] = velocity
         RN[...] = stored.astype(BF16)
 
-    def near_rows():
-        for o, side in ((3, "m-"), (1, "m+")):
-            for j in {"m-": (4, 5, 6, 7), "m+": (0, 1, 2, 3)}[side]:
-                arrived(master(o, j), (side, j))
-            arrived(wv.at[zo[o]], f"w{o}")
-            recast(o)
-
-    def far_rows():
-        for j in range(8):
-            arrived(master(2, j), ("m2", j))
-        arrived(wv.at[zo[2]], "w2")
-        recast(2)
-
     def take(kind, h, o, p, e):
         if (o, p, e) == OWN:
             {"D": own_down, "U": own_up}[kind](h)
@@ -385,7 +396,14 @@
             arrived(view(kind, h, o, p, e), (kind, h, (o, p, e)))
         forward((kind, h, o, p, e), "c")
 
-    extra = {"weights": weights, "swap": swap, "local": local_steps, "near": near_rows, "far": far_rows}
+    extra = {
+        "project": project,
+        "master": project_master,
+        "weights": weights,
+        "swap": swap,
+        "local": local_steps,
+        "recast": recast,
+    }
     for step in plan():
         if step[0] == "take":
             take(*step[1])
@@ -396,7 +414,7 @@
         elif step[0] == "relay":
             relay_master(step[1], step[2])
         else:
-            extra[step[1]]()
+            extra[step[1]](*step[2:])
 
     for i, ref in enumerate((RD, RU)):
         landed = ref.at[pl.ds(0, 32)]

time: 50.7 us -> 50.6 us (level)
  no operation moved by 1% of the time
where the time goes in v3:
time: 50.6 us; the launch traced here: 50.5 us
  Pallas kernels  49.9 us (99%)
  between operations  0.66 us (1%)
    pallas_call x1, Pallas kernels, body(): pl.pallas_call(exchange, out_shape=tuple((pltpu.VMEM(shape, dtype) for sh...  45.3 us
    pallas_call x1, Pallas kernels, body(): pl.pallas_call(flush, out_shape=tuple((jax.ShapeDtypeStruct(shape, dtype)...  4.61 us

profile of v3, /device:TPU:1, one launch (start us, length us, event | category | flops | bytes accessed | tf_op | source)
XLA Modules:
  0.0 50.5 jit_solution(14650243615866080835)
XLA Ops:
  0.6 45.3 %exchange.1 = (bf16[64,16,2048]{2,1,0:T(8,128)(2,1)S(1)}, bf16[64,32,1024]{2,1,0:T(8,128)(2,1)S(1)}, bf16[16,64,1024]{2,1,0:T(8,128)(2,1)S(1)}, bf16[2,1024]{1,0...) custom-call(bf16[4,16,16,2048]{3,2,1,0:T(8,128)(2,1)} %bitcast.20, ...), custom_call_target="tpu_custom_call" | custom-call | tf_op jit(solution)/shard_map/exchange/pallas_call | solution.py:493
  45.9 4.6 %flush.1 = (bf16[64,16,2048]{2,1,0:T(8,128)(2,1)}, bf16[64,32,1024]{2,1,0:T(8,128)(2,1)}, bf16[16,64,1024]{2,1,0:T(8,128)(2,1)}, bf16[2,1024]{1,0:T(2,128)(2,1)}...) custom-call(bf16[64,16,2048]{2,1,0:T(8,128)(2,1)S(1)} %get-tuple-ele, ...), custom_call_target="tpu_custom_call" | custom-call | tf_op jit(solution)/shard_map/flush/pallas_call | solution.py:545
